TPU v7x, 32 devices: a whole 2x2x4 slice. The times are simulated.
32 devices in a mesh: dp: 8 (over z, y), tm: 4 (over x, core).
Axes of the slice: x: 2, y: 2, z: 4, core: 2. Of those that a mesh axis runs over, the one named last changes fastest.
Arguments:
- currents: bfloat16 [8, 32, 128, 1280], P('dp', 'tm'), may hold values from -4 to 4, as said below
- mixing: float32 [32, 32], replicated, may hold values from -1 to 1, as said below
- threshold: float32 [32], replicated, may hold values from -4 to 4, as said below
- weight: bfloat16 [1280, 1280], replicated, may hold values from -0.15625 to 0.15625
- bias: float32 [1280], replicated, may hold values from -3 to 3
- cotangent: bfloat16 [8, 32, 128, 1280], P('dp', 'tm'), may hold values from -6 to 6
Outputs:
- output: bfloat16 [8, 32, 128, 1280], P('dp', 'tm')
- current_grad: bfloat16 [8, 32, 128, 1280], P('dp', 'tm')
- weight_grad: bfloat16 [1280, 1280], P(('dp', 'tm'))
- mixing_grad: float32 [32, 32], replicated
- threshold_grad: float32 [32], replicated
- bias_grad: float32 [1280], replicated
Inputs may be any that keep to these rules, and one draw needn't show every extreme that they name: `currents`: every entry is a multiple of 1/16. `mixing`: every entry is a multiple of 1/16. threshold: every entry is an odd multiple of 1/512, so that every membrane value (a multiple of 1/256) lies at least 1/512 from its threshold.
All inputs are finite; a program needn't handle non-finite values.
Results may differ from a plain program's by a relative error of at most 0.0049.
Values may be sent and summed in bfloat16 or wider, within the bound.
No kernel may reach another device: no remote copies, remote signals or barrier semaphores. Data moves between devices by JAX's collectives and lax.ppermute only.
A program may use at most 128 MiB of HBM per device.

v0:
```python
import jax
import jax.numpy as jnp
from jax import lax
from jax.sharding import PartitionSpec as P


def neuron_forward(currents, mixing, threshold):
    highest = lax.Precision.HIGHEST
    wide_cur = currents.astype(jnp.float32)
    membrane = jnp.einsum("tj,ijnd->itnd", mixing, wide_cur, precision=highest)
    shifted = membrane - threshold[None, :, None, None]
    spikes = (shifted > 0).astype(jnp.bfloat16)
    sigmoid_val = jax.nn.sigmoid(shifted)
    surrogate = sigmoid_val * (1.0 - sigmoid_val)
    return (wide_cur, spikes, surrogate)


def neuron_backward(spike_grad, surrogate, mixing, wide_cur):
    highest = lax.Precision.HIGHEST
    membrane_grad = spike_grad.astype(jnp.float32) * surrogate
    input_grad = jnp.einsum("tj,itnd->ijnd", mixing, membrane_grad, precision=highest).astype(
        jnp.bfloat16
    )
    mixing_term = jnp.einsum("itnd,ijnd->tj", membrane_grad, wide_cur, precision=highest)
    threshold_term = -jnp.sum(membrane_grad, axis=(0, 2, 3))
    return (input_grad, mixing_term, threshold_term)


def body(currents, mixing, threshold, weight, bias, cotangent):
    shape = cotangent.shape
    width = shape[3]
    tok_cur = lax.all_to_all(currents, "tm", split_axis=2, concat_axis=1, tiled=True)
    wide_cur, tok_spikes, surrogate = neuron_forward(tok_cur, mixing, threshold)
    spikes = lax.all_to_all(tok_spikes, "tm", split_axis=1, concat_axis=2, tiled=True)
    spike_rows = spikes.reshape(-1, width)
    grad_rows = cotangent.reshape(-1, width)
    output = (
        (jnp.dot(spike_rows, weight, preferred_element_type=jnp.float32) + bias)
        .astype(jnp.bfloat16)
        .reshape(shape)
    )
    spike_grad = (
        jnp.einsum("re,de->rd", grad_rows, weight, preferred_element_type=jnp.float32)
        .astype(jnp.bfloat16)
        .reshape(shape)
    )
    weight_term = jnp.einsum("rd,re->de", spike_rows, grad_rows, preferred_element_type=jnp.float32)
    bias_term = jnp.sum(grad_rows.astype(jnp.float32), axis=0)
    tok_grad = lax.all_to_all(spike_grad, "tm", split_axis=2, concat_axis=1, tiled=True)
    tok_cgrad, mixing_term, threshold_term = neuron_backward(tok_grad, surrogate, mixing, wide_cur)
    current_grad = lax.all_to_all(tok_cgrad, "tm", split_axis=1, concat_axis=2, tiled=True)
    weight_sum = lax.psum_scatter(weight_term, ("dp", "tm"), scatter_dimension=0, tiled=True)
    mixing_grad, threshold_grad, bias_grad = lax.psum(
        (mixing_term, threshold_term, bias_term), ("dp", "tm")
    )
    return (
        output,
        current_grad,
        weight_sum.astype(jnp.bfloat16),
        mixing_grad,
        threshold_grad,
        bias_grad,
    )


def solution(mesh):
    return jax.shard_map(
        body,
        mesh=mesh,
        in_specs=(P("dp", "tm", None, None), P(), P(), P(), P(), P("dp", "tm", None, None)),
        out_specs=(
            P("dp", "tm", None, None),
            P("dp", "tm", None, None),
            P(("dp", "tm"), None),
            P(),
            P(),
            P(),
        ),
        check_vma=False,
    )
```

profile of v0, /device:TPU:0, one launch (start us, length us, event | category | flops | bytes accessed | tf_op | source)
XLA Modules:
  0.0 300.1 jit_solution(4259585015621780677)
XLA Ops:
  7.2 0.0 copy-start
  7.2 1.9 copy-done
  9.1 5.3 %convolution_convert_fusion = bf16[1024,1280]{1,0:T(8,128)(2,1)S(1)} fusion(bf16[1024,1280]{1,0:T(8,128)(2,1)} %bitcast.77, bf16[1280,1280]{1,0:T(8,128)(2,1)S(1)} %copy-done), kind=kOutput, calls=%fused_computation.12 | convolution fusion | flops 3356753920 | bytes 8519680 | tf_op jit(solution)/shard_map/re,de->rd/dot_general | solution.py:43
  14.4 2.9 copy.33
  17.4 4.5 %all-to-all-start.2 = ((bf16[1,8,128,1280]{3,1,0,2:T(8,128)(2,1)}), bf16[1,8,128,1280]{3,1,0,2:T(8,128)(2,1)}, u32[]{:S(2)}, u32[]{:S(2)}) async-start(bf16[1,8,128,1280]{3,1,0,2:T(8,128)(2,1)} %copy.33), calls=%async_computation.2 | async-start | bytes 5242880 | tf_op jit(solution)/shard_map/all_to_all | solution.py:49
  21.9 4.7 %copy.29 = bf16[1,8,128,1280]{3,1,0,2:T(8,128)(2,1)} copy(bf16[1,8,128,1280]{3,2,1,0:T(8,128)(2,1)} %param.6) | data formatting | bytes 5242880 | tf_op args[0]
  26.6 27.3 %all-to-all-done.2 = bf16[1,8,128,1280]{3,1,0,2:T(8,128)(2,1)} async-done(((bf16[1,8,128,1280]{3,1,0,2:T(8,128)(2,1)}), bf16[1,8,128,1280]{3,1,0,2:T(8,128)(2,1)}, u32[]{:S(2)}, u32[]{:S(2)}) %all-to-all-start.2) | async-done | bytes 2621472 | tf_op jit(solution)/shard_map/all_to_all | solution.py:49
  53.9 4.6 %all-to-all-start = ((bf16[1,8,128,1280]{3,1,0,2:T(8,128)(2,1)}), bf16[1,8,128,1280]{3,1,0,2:T(8,128)(2,1)}, u32[]{:S(2)}, u32[]{:S(2)}) async-start(bf16[1,8,128,1280]{3,1,0,2:T(8,128)(2,1)} %copy.29), calls=%async_computation | async-start | bytes 5242880 | tf_op jit(solution)/shard_map/all_to_all | solution.py:32
  58.5 0.0 reduce-scatter.2.cloned.1.call-start
  58.5 2.2 copy.34
  60.7 0.0 copy-start.4
  60.8 0.0 copy-start.5
  60.8 3.0 convert_bitcast_fusion
  63.7 26.1 %all-to-all-done = bf16[1,8,128,1280]{3,1,0,2:T(8,128)(2,1)} async-done(((bf16[1,8,128,1280]{3,1,0,2:T(8,128)(2,1)}), bf16[1,8,128,1280]{3,1,0,2:T(8,128)(2,1)}, u32[]{:S(2)}, u32[]{:S(2)}) %all-to-all-start) | async-done | bytes 2621472 | tf_op jit(solution)/shard_map/all_to_all | solution.py:32
  89.8 0.0 copy-done.4
  89.8 0.0 copy-done.5
  89.8 10.1 %fusion.24 = (f32[32]{0:T(128)S(1)}, f32[1,32,32,1280]{3,1,2,0:T(8,128)}, f32[32,1280,32]{1,2,0:T(8,128)S(1)}) fusion(f32[32]{0:T(128)S(1)} %copy-done.5, f32[1,4,8,32,1280]{4,3,1,2,0:T(8,128)} %convert_bitcast_fusion, f32[32,32]{1,0:T(8,128)S(1)} %copy-done.4, bf16[1,8,4,32,1280]{4,1,3,2,0:T(8,128)(2,1)} %bitcast), kind=kOutput, calls=%fused_computation.23 | convolution fusion | flops 513802208 | bytes 18354432 | tf_op jit(solution)/shard_map/tj,ijnd->itnd/dot_general | solution.py:10
  100.0 0.8 fusion.11
  100.8 1.4 copy.31
  102.2 33.8 %all_to_all.57 = bf16[1,32,32,1280]{3,2,0,1:T(8,128)(2,1)S(1)} all-to-all(bf16[1,32,32,1280]{3,2,0,1:T(8,128)(2,1)S(1)} %copy.31), channel_id=1, replica_groups=mesh['dp'=8,'tm'=4] {'tm'}, dimensions={1} | all-to-all | bytes 5242880 | tf_op jit(solution)/shard_map/all_to_all | solution.py:34
  136.0 0.0 copy-start.1
  136.0 0.2 copy.32
  136.2 0.0 copy-start.2
  136.3 1.5 copy-done.2
  137.7 1.0 copy-done.1
  138.7 5.6 %fusion.26 = f32[1280,1280]{1,0:T(8,128)} fusion(bf16[1024,1280]{1,0:T(8,128)(2,1)S(1)} %bitcast.79, bf16[1024,1280]{1,0:T(8,128)(2,1)S(1)} %bitcast.78), kind=kOutput, calls=%fused_computation.24 | convolution fusion | flops 3355443200 | bytes 11796480 | tf_op jit(solution)/shard_map/rd,re->de/dot_general | solution.py:47
  144.3 0.0 reduce-scatter.2.cloned.1.call-update
  144.3 7.1 %fusion.8 = bf16[1,32,32,1280]{3,1,2,0:T(8,128)(2,1)S(1)} fusion(f32[1,32,32,1280]{3,1,2,0:T(8,128)} %get-tuple-element.10, f32[32,32]{1,0:T(8,128)S(1)} %copy-done.4), kind=kOutput, calls=%fused_computation.13 | convolution fusion | flops 504627200 | bytes 7868416 | tf_op jit(solution)/shard_map/tj,itnd->ijnd/dot_general | solution.py:21
  151.4 2.9 copy.37
  154.3 4.6 %all-to-all-start.3 = ((bf16[1,32,32,1280]{3,2,0,1:T(8,128)(2,1)}), bf16[1,32,32,1280]{3,2,0,1:T(8,128)(2,1)}, u32[]{:S(2)}, u32[]{:S(2)}) async-start(bf16[1,32,32,1280]{3,2,0,1:T(8,128)(2,1)} %copy.37), calls=%async_computation.3 | async-start | bytes 5242880 | tf_op jit(solution)/shard_map/all_to_all | solution.py:51
  158.9 2.2 convert_reduce_fusion
  161.1 5.8 %fusion.17 = f32[32,32]{1,0:T(8,128)S(1)} fusion(bf16[1,8,4,32,1280]{4,1,3,2,0:T(8,128)(2,1)} %bitcast, f32[1,32,32,1280]{3,1,2,0:T(8,128)} %get-tuple-element.10), kind=kOutput, calls=%fused_computation.20 | convolution fusion | flops 503316480 | bytes 7868416 | tf_op jit(solution)/shard_map/itnd,ijnd->tj/dot_general | solution.py:24
  166.9 89.1 %all-reduce = (f32[32,32]{1,0:T(8,128)}, f32[32]{0:T(128)}, f32[1280]{0:T(1024)}) all-reduce(f32[32,32]{1,0:T(8,128)S(1)} %fusion.17, f32[32]{0:T(128)S(1)} %neg.8, f32[1280]{0:T(1024)S(1)} %convert_reduce_fusion), channel_id=1, replica_groups=mesh['dp'=8,'tm'=4] {'dp','tm'}, use_global_device_ids=true, to_apply=%region_1.0 | all-reduce | flops 2336 | bytes 18688 | tf_op jit(solution)/shard_map/psum | solution.py:53
  256.1 0.0 all-to-all-done.3
  256.1 0.0 copy-start.3
  256.1 0.0 copy-start.6
  256.1 3.6 %copy.38 = bf16[1,8,4,32,1280]{4,3,2,1,0:T(8,128)(2,1)} copy(bf16[1,8,4,32,1280]{4,3,1,2,0:T(8,128)(2,1)} %bitcast.21) | data formatting | bytes 5242880 | tf_op jit(solution)/shard_map/all_to_all | solution.py:51
  259.7 0.0 copy-done.3
  259.7 0.0 copy-done.6
  259.7 4.8 %add_convert_fusion = bf16[1024,1280]{1,0:T(8,128)(2,1)} fusion(bf16[1024,1280]{1,0:T(8,128)(2,1)S(1)} %bitcast.80, bf16[1280,1280]{1,0:T(8,128)(2,1)S(1)} %copy-done, f32[1280]{0:T(1024)S(1)} %copy-done.6), kind=kOutput, calls=%fused_computation.9 | convolution fusion | flops 3358064640 | bytes 8524800 | tf_op jit(solution)/shard_map/dot_general | solution.py:38
  264.5 27.2 %reduce-scatter.2.cloned.1.call-done = f32[40,1280]{1,0:T(8,128)} async-done(((f32[1280,1280]{1,0:T(8,128)}), f32[40,1280]{1,0:T(8,128)}) %reduce-scatter.2.cloned.1.call-update) | async-done | bytes 204816 | tf_op jit(solution)/shard_map/reduce_scatter | solution.py:52
  291.7 1.6 convert_element_type.60
  (1 shorter events, 0.0 us)
Async XLA Ops:
  7.2 1.9 copy-start
  17.4 36.5 %all-to-all-start.2 = ((bf16[1,8,128,1280]{3,1,0,2:T(8,128)(2,1)}), bf16[1,8,128,1280]{3,1,0,2:T(8,128)(2,1)}, u32[]{:S(2)}, u32[]{:S(2)}) async-start(bf16[1,8,128,1280]{3,1,0,2:T(8,128)(2,1)} %copy.33), calls=%async_computation.2 | async-start | bytes 5242880 | tf_op jit(solution)/shard_map/all_to_all | solution.py:49
  53.9 35.9 %all-to-all-start = ((bf16[1,8,128,1280]{3,1,0,2:T(8,128)(2,1)}), bf16[1,8,128,1280]{3,1,0,2:T(8,128)(2,1)}, u32[]{:S(2)}, u32[]{:S(2)}) async-start(bf16[1,8,128,1280]{3,1,0,2:T(8,128)(2,1)} %copy.29), calls=%async_computation | async-start | bytes 5242880 | tf_op jit(solution)/shard_map/all_to_all | solution.py:32
  58.5 233.2 %reduce-scatter.2.cloned.1.call-start = ((), (), s32[]{:S(2)}) async-start(), calls=%async_computation.5 | async-start | bytes 6758400 | tf_op jit(solution)/shard_map/reduce_scatter | solution.py:52
  60.7 29.1 %copy-start.4 = (f32[32,32]{1,0:T(8,128)S(1)}, f32[32,32]{1,0:T(8,128)}, u32[]{:S(2)}) copy-start(f32[32,32]{1,0:T(8,128)} %param.7) | copy-start | bytes 12292
  60.8 29.1 %copy-start.5 = (f32[32]{0:T(128)S(1)}, f32[32]{0:T(128)}, u32[]{:S(2)}) copy-start(f32[32]{0:T(128)} %param.8) | copy-start | bytes 388
  136.0 2.7 copy-start.1
  136.2 1.5 copy-start.2
  154.3 101.7 %all-to-all-start.3 = ((bf16[1,32,32,1280]{3,2,0,1:T(8,128)(2,1)}), bf16[1,32,32,1280]{3,2,0,1:T(8,128)(2,1)}, u32[]{:S(2)}, u32[]{:S(2)}) async-start(bf16[1,32,32,1280]{3,2,0,1:T(8,128)(2,1)} %copy.37), calls=%async_computation.3 | async-start | bytes 5242880 | tf_op jit(solution)/shard_map/all_to_all | solution.py:51
  256.1 3.6 %copy-start.3 = (bf16[1,8,4,32,1280]{4,3,2,1,0:T(8,128)(2,1)S(1)}, bf16[1,8,4,32,1280]{4,3,2,1,0:T(8,128)(2,1)}, u32[]{:S(2)}) copy-start(bf16[1,8,4,32,1280]{4,3,2,1,0:T(8,128)(2,1)} %copy-done.2) | copy-start | bytes 7864324
  256.1 3.6 %copy-start.6 = (f32[1280]{0:T(1024)S(1)}, f32[1280]{0:T(1024)}, u32[]{:S(2)}) copy-start(f32[1280]{0:T(1024)} %param.10) | copy-start | bytes 15364
Sparse Core Ops, SparseCore 0:
  144.4 147.2 reduce-scatter.1
where the time goes:
time: 301 us; the launch traced here: 300 us
  blocking collectives  123 us (41%)
  waiting for transfers between devices  80.6 us (27%)
  matrix products  38.7 us (13%)
  local copies, waits for them, and re-layouts  22.4 us (7%)
  between operations  14.2 us (5%)
  starting transfers between devices  13.7 us (5%)
  other arithmetic  7.52 us (2%)
    psum x1, blocking collectives, body(): lax.psum((mixing_term, threshold_term, bias_term), ('dp', 'tm'))  89.1 us
    all_to_all x1, blocking collectives, body(): lax.all_to_all(tok_spikes, 'tm', split_axis=1, concat_axis=2, tiled=True)  33.8 us
    all_to_all x1, waiting for transfers between devices, body(): lax.all_to_all(spike_grad, 'tm', split_axis=2, concat_axis=1, tiled=True)  27.3 us
    reduce_scatter x1, waiting for transfers between devices, body(): lax.psum_scatter(weight_term, ('dp', 'tm'), scatter_dimension=0, tiled=True)  27.2 us
    all_to_all x1, waiting for transfers between devices, body(): lax.all_to_all(currents, 'tm', split_axis=2, concat_axis=1, tiled=True)  26.1 us
    dot_general x1, matrix products, neuron_forward(): membrane = jnp.einsum('tj,ijnd->itnd', mixing, wide_cur, precision=highest)  10.1 us
    unnamed x15, local copies, waits for them, and re-layouts  9.07 us
    dot_general x1, matrix products, neuron_backward(): jnp.einsum('tj,itnd->ijnd', mixing, membrane_grad, precision=highest)  7.08 us
  transfers between devices with their start and end apart: 4, of which 3 were waited for; matrix products, arithmetic and copies ran while one was open for 12% of the time, Pallas kernels for 0%

commit v1 on v0

--- a/solution.py
+++ b/solution.py
@@ -2,6 +2,26 @@
 import jax.numpy as jnp
 from jax import lax
 from jax.sharding import PartitionSpec as P
+
+
+def detail_arrays(chunk):
+    dev_axis = "tm"
+    upper, reached = (jax.lax.axis_size(dev_axis), jax.lax.axis_index(dev_axis))
+    b_now = chunk.shape[2] // upper
+    part_now = list(chunk.shape)
+    part_now[2] = b_now
+    even = part_now[1]
+    part_now[1] = even * upper
+    oldest = jnp.zeros(part_now, chunk.dtype)
+    for c in range(upper):
+        arr_next = lax.dynamic_slice_in_dim(chunk, (reached ^ c) * b_now, b_now, axis=2)
+        if c:
+            pages = []
+            for hop_no in range(upper):
+                pages.append((hop_no, hop_no ^ c))
+            arr_next = jax.lax.ppermute(arr_next, dev_axis, perm=pages)
+        oldest = lax.dynamic_update_slice_in_dim(oldest, arr_next, (reached ^ c) * even, axis=1)
+    return oldest
 
 
 def neuron_forward(currents, mixing, threshold):
@@ -46,7 +66,7 @@
     )
     weight_term = jnp.einsum("rd,re->de", spike_rows, grad_rows, preferred_element_type=jnp.float32)
     bias_term = jnp.sum(grad_rows.astype(jnp.float32), axis=0)
-    tok_grad = lax.all_to_all(spike_grad, "tm", split_axis=2, concat_axis=1, tiled=True)
+    tok_grad = detail_arrays(spike_grad)
     tok_cgrad, mixing_term, threshold_term = neuron_backward(tok_grad, surrogate, mixing, wide_cur)
     current_grad = lax.all_to_all(tok_cgrad, "tm", split_axis=1, concat_axis=2, tiled=True)
     weight_sum = lax.psum_scatter(weight_term, ("dp", "tm"), scatter_dimension=0, tiled=True)

time: 301 us -> 288 us (0.957)
  waiting for transfers between devices: 80.6 us -> 63.3 us
  local copies, waits for them, and re-layouts: 22.4 us -> 30.7 us
    ppermute x0 -> x3, waiting for transfers between devices: none -> 36.1 us  [detail_arrays(): arr_next = jax.lax.ppermute(arr_next, dev_axis, perm=pages)]
    all_to_all x1 -> x0, waiting for transfers between devices: 27.3 us -> none  [body(): lax.all_to_all(spike_grad, 'tm', split_axis=2, concat_axis=1, tiled=True)]
    all_to_all x1, waiting for transfers between devices: 26.1 us -> 0.01 us  [body(): lax.all_to_all(currents, 'tm', split_axis=2, concat_axis=1, tiled=True)]
    dynamic_update_slice x0 -> x4, local copies, waits for them, and re-layouts: none -> 7.1 us  [detail_arrays(): lax.dynamic_update_slice_in_dim(oldest, arr_next, (reached ^ c) * even, a...]
    all_to_all x1 -> x0, starting transfers between devices: 4.55 us -> none  [body(): lax.all_to_all(spike_grad, 'tm', split_axis=2, concat_axis=1, tiled=True)]
    ppermute x0 -> x3, starting transfers between devices: none -> 3.06 us  [detail_arrays(): arr_next = jax.lax.ppermute(arr_next, dev_axis, perm=pages)]
    unnamed x15 -> x20, local copies, waits for them, and re-layouts: 9.07 us -> 10.9 us
  transfers between devices with their start and end apart: 4 -> 6, of which waited for: 3 -> 3; matrix products, arithmetic and copies ran while one was open for 12% -> 17% of each run, Pallas kernels for 0% -> 0%
where the time goes in v1:
time: 288 us; the launch traced here: 287 us
  blocking collectives  123 us (43%)
  waiting for transfers between devices  63.3 us (22%)
  matrix products  38.8 us (13%)
  local copies, waits for them, and re-layouts  30.7 us (11%)
  between operations  14.1 us (5%)
  starting transfers between devices  12.2 us (4%)
  other arithmetic  4.57 us (2%)
    psum x1, blocking collectives, body(): lax.psum((mixing_term, threshold_term, bias_term), ('dp', 'tm'))  89.6 us
    ppermute x3, waiting for transfers between devices, detail_arrays(): arr_next = jax.lax.ppermute(arr_next, dev_axis, perm=pages)  36.1 us
    all_to_all x1, blocking collectives, body(): lax.all_to_all(tok_spikes, 'tm', split_axis=1, concat_axis=2, tiled=True)  33.8 us
    reduce_scatter x1, waiting for transfers between devices, body(): lax.psum_scatter(weight_term, ('dp', 'tm'), scatter_dimension=0, tiled=True)  27.2 us
    unnamed x20, local copies, waits for them, and re-layouts  10.9 us
    dot_general x1, matrix products, neuron_forward(): membrane = jnp.einsum('tj,ijnd->itnd', mixing, wide_cur, precision=highest)  8.71 us
    dynamic_update_slice x4, local copies, waits for them, and re-layouts, detail_arrays(): lax.dynamic_update_slice_in_dim(oldest, arr_next, (reached ^ c) * even, a...  7.1 us
    dot_general x1, matrix products, neuron_backward(): jnp.einsum('tj,itnd->ijnd', mixing, membrane_grad, precision=highest)  7.08 us
  transfers between devices with their start and end apart: 6, of which 3 were waited for; matrix products, arithmetic and copies ran while one was open for 17% of the time, Pallas kernels for 0%

profile of v1, /device:TPU:0, one launch (start us, length us, event | category | flops | bytes accessed | tf_op | source)
XLA Modules:
  0.0 287.1 jit_solution(11610301422428854933)
XLA Ops:
  7.2 0.0 copy-start
  7.2 4.8 %copy.33 = bf16[1,8,128,1280]{3,1,0,2:T(8,128)(2,1)} copy(bf16[1,8,128,1280]{3,2,1,0:T(8,128)(2,1)} %param.6) | data formatting | bytes 5242880 | tf_op args[0]
  12.0 4.6 %all-to-all-start = ((bf16[1,8,128,1280]{3,1,0,2:T(8,128)(2,1)}), bf16[1,8,128,1280]{3,1,0,2:T(8,128)(2,1)}, u32[]{:S(2)}, u32[]{:S(2)}) async-start(bf16[1,8,128,1280]{3,1,0,2:T(8,128)(2,1)} %copy.33), calls=%async_computation | async-start | bytes 5242880 | tf_op jit(solution)/shard_map/all_to_all | solution.py:52
  16.6 0.0 reduce-scatter.2.cloned.1.call-start
  16.6 0.0 copy-done
  16.6 6.8 %convolution_convert_fusion = bf16[1024,1280]{1,0:T(8,128)(2,1)} fusion(bf16[1024,1280]{1,0:T(8,128)(2,1)} %bitcast.69, bf16[1280,1280]{1,0:T(8,128)(2,1)S(1)} %copy-done), kind=kOutput, calls=%fused_computation.11 | convolution fusion | flops 3356753920 | bytes 8519680 | tf_op jit(solution)/shard_map/re,de->rd/dot_general | solution.py:63
  23.4 2.7 constant_dynamic-slice_fusion
  26.1 1.2 copy.47
  27.3 0.5 collective-permute-start
  27.8 1.2 copy.48
  29.0 2.5 collective-permute-start.1
  31.5 1.2 copy.49
  32.7 0.1 collective-permute-start.2
  32.8 0.0 copy-start.1
  32.8 1.8 broadcast_in_dim.2
  34.6 0.0 copy-done.1
  34.6 0.0 copy-start.5
  34.6 0.0 copy-start.6
  34.6 1.2 copy_dynamic-update-slice_fusion
  35.8 0.0 collective-permute-done
  35.8 2.0 constant_dynamic-update-slice_fusion.2
  37.8 25.7 %collective-permute-done.1 = bf16[1,8,32,1280]{3,1,2,0:T(8,128)(2,1)} collective-permute-done((bf16[1,8,32,1280]{3,1,2,0:T(8,128)(2,1)}, bf16[1,8,32,1280]{3,1,2,0:T(8,128)(2,1)}, u32[]{:S(2)}, u32[]{:S(2)}) %collective-permute-start.1) | collective-permute-done | bytes 655392 | tf_op jit(solution)/shard_map/ppermute | solution.py:22
  63.4 2.0 constant_dynamic-update-slice_fusion.1
  65.4 10.4 %collective-permute-done.2 = bf16[1,8,32,1280]{3,1,2,0:T(8,128)(2,1)} collective-permute-done((bf16[1,8,32,1280]{3,1,2,0:T(8,128)(2,1)}, bf16[1,8,32,1280]{3,1,2,0:T(8,128)(2,1)}, u32[]{:S(2)}, u32[]{:S(2)}) %collective-permute-start.2) | collective-permute-done | bytes 655392 | tf_op jit(solution)/shard_map/ppermute | solution.py:22
  75.8 2.0 constant_dynamic-update-slice_fusion
  77.8 0.0 all-to-all-done
  77.8 0.0 copy-done.5
  77.8 0.0 copy-done.6
  77.8 8.7 %fusion.24 = (f32[32]{0:T(128)S(1)}, f32[1,32,32,1280]{3,1,2,0:T(8,128)}, f32[32,1280,32]{1,2,0:T(8,128)S(1)}) fusion(f32[32]{0:T(128)S(1)} %copy-done.6, bf16[1,32,32,1280]{3,1,2,0:T(8,128)(2,1)} %constant_dynamic-update-slice_fusion, f32[32,32]{1,0:T(8,128)S(1)} %copy-done.5, bf16[1,8,4,32,1280]{4,1,3,2,0:T(8,128)(2,1)} %bitcast), kind=kOutput, calls=%fused_computation.30 | convolution fusion | flops 515112928 | bytes 15732992 | tf_op jit(solution)/shard_map/tj,ijnd->itnd/dot_general | solution.py:30
  86.5 0.8 fusion.11
  87.3 1.4 copy.35
  88.7 33.8 %all_to_all.48 = bf16[1,32,32,1280]{3,2,0,1:T(8,128)(2,1)S(1)} all-to-all(bf16[1,32,32,1280]{3,2,0,1:T(8,128)(2,1)S(1)} %copy.35), channel_id=1, replica_groups=mesh['dp'=8,'tm'=4] {'tm'}, dimensions={1} | all-to-all | bytes 5242880 | tf_op jit(solution)/shard_map/all_to_all | solution.py:54
  122.5 0.0 copy-start.2
  122.5 0.2 copy.36
  122.8 0.0 copy-start.3
  122.8 1.5 copy-done.3
  124.2 1.0 copy-done.2
  125.2 5.6 %fusion.26 = f32[1280,1280]{1,0:T(8,128)} fusion(bf16[1024,1280]{1,0:T(8,128)(2,1)S(1)} %bitcast.72, bf16[1024,1280]{1,0:T(8,128)(2,1)S(1)} %bitcast.70), kind=kOutput, calls=%fused_computation.31 | convolution fusion | flops 3355443200 | bytes 11796480 | tf_op jit(solution)/shard_map/rd,re->de/dot_general | solution.py:67
  130.8 0.0 reduce-scatter.2.cloned.1.call-update
  130.8 7.1 %fusion.8 = bf16[1,32,32,1280]{3,1,2,0:T(8,128)(2,1)S(1)} fusion(f32[1,32,32,1280]{3,1,2,0:T(8,128)} %get-tuple-element.10, f32[32,32]{1,0:T(8,128)S(1)} %copy-done.5), kind=kOutput, calls=%fused_computation.12 | convolution fusion | flops 504627200 | bytes 7868416 | tf_op jit(solution)/shard_map/tj,itnd->ijnd/dot_general | solution.py:41
  137.9 2.9 %copy.42 = bf16[1,32,32,1280]{3,2,0,1:T(8,128)(2,1)} copy(bf16[1,32,32,1280]{3,1,2,0:T(8,128)(2,1)S(1)} %fusion.8) | data formatting | bytes 5242880 | tf_op jit(solution)/shard_map/convert_element_type | solution.py:41
  140.9 4.6 %all-to-all-start.2 = ((bf16[1,32,32,1280]{3,2,0,1:T(8,128)(2,1)}), bf16[1,32,32,1280]{3,2,0,1:T(8,128)(2,1)}, u32[]{:S(2)}, u32[]{:S(2)}) async-start(bf16[1,32,32,1280]{3,2,0,1:T(8,128)(2,1)} %copy.42), calls=%async_computation.2 | async-start | bytes 5242880 | tf_op jit(solution)/shard_map/all_to_all | solution.py:71
  145.4 2.2 convert_reduce_fusion
  147.6 5.8 %fusion.17 = f32[32,32]{1,0:T(8,128)S(1)} fusion(bf16[1,8,4,32,1280]{4,1,3,2,0:T(8,128)(2,1)} %bitcast, f32[1,32,32,1280]{3,1,2,0:T(8,128)} %get-tuple-element.10), kind=kOutput, calls=%fused_computation.19 | convolution fusion | flops 503316480 | bytes 7868416 | tf_op jit(solution)/shard_map/itnd,ijnd->tj/dot_general | solution.py:44
  153.5 89.6 %all-reduce = (f32[32,32]{1,0:T(8,128)}, f32[32]{0:T(128)}, f32[1280]{0:T(1024)}) all-reduce(f32[32,32]{1,0:T(8,128)S(1)} %fusion.17, f32[32]{0:T(128)S(1)} %neg.8, f32[1280]{0:T(1024)S(1)} %convert_reduce_fusion), channel_id=1, replica_groups=mesh['dp'=8,'tm'=4] {'dp','tm'}, use_global_device_ids=true, to_apply=%region_1.0 | all-reduce | flops 2336 | bytes 18688 | tf_op jit(solution)/shard_map/psum | solution.py:73
  243.0 0.0 all-to-all-done.2
  243.0 0.0 copy-start.4
  243.0 0.0 copy-start.7
  243.0 3.6 %copy.43 = bf16[1,8,4,32,1280]{4,3,2,1,0:T(8,128)(2,1)} copy(bf16[1,8,4,32,1280]{4,3,1,2,0:T(8,128)(2,1)} %bitcast.18) | data formatting | bytes 5242880 | tf_op jit(solution)/shard_map/all_to_all | solution.py:71
  246.7 0.0 copy-done.4
  246.7 0.0 copy-done.7
  246.7 4.8 %add_convert_fusion = bf16[1024,1280]{1,0:T(8,128)(2,1)} fusion(bf16[1024,1280]{1,0:T(8,128)(2,1)S(1)} %bitcast.73, bf16[1280,1280]{1,0:T(8,128)(2,1)S(1)} %copy-done, f32[1280]{0:T(1024)S(1)} %copy-done.7), kind=kOutput, calls=%fused_computation.8 | convolution fusion | flops 3358064640 | bytes 8524800 | tf_op jit(solution)/shard_map/dot_general | solution.py:58
  251.5 27.2 %reduce-scatter.2.cloned.1.call-done = f32[40,1280]{1,0:T(8,128)} async-done(((f32[1280,1280]{1,0:T(8,128)}), f32[40,1280]{1,0:T(8,128)}) %reduce-scatter.2.cloned.1.call-update) | async-done | bytes 204816 | tf_op jit(solution)/shard_map/reduce_scatter | solution.py:72
  278.7 1.6 convert_element_type.40
  (1 shorter events, 0.0 us)
Async XLA Ops:
  7.2 9.4 %copy-start = (bf16[1280,1280]{1,0:T(8,128)(2,1)S(1)}, bf16[1280,1280]{1,0:T(8,128)(2,1)}, u32[]{:S(2)}) copy-start(bf16[1280,1280]{1,0:T(8,128)(2,1)} %param.9) | copy-start | bytes 9830404
  12.0 65.8 %all-to-all-start = ((bf16[1,8,128,1280]{3,1,0,2:T(8,128)(2,1)}), bf16[1,8,128,1280]{3,1,0,2:T(8,128)(2,1)}, u32[]{:S(2)}, u32[]{:S(2)}) async-start(bf16[1,8,128,1280]{3,1,0,2:T(8,128)(2,1)} %copy.33), calls=%async_computation | async-start | bytes 5242880 | tf_op jit(solution)/shard_map/all_to_all | solution.py:52
  16.6 262.1 %reduce-scatter.2.cloned.1.call-start = ((), (), s32[]{:S(2)}) async-start(), calls=%async_computation.4 | async-start | bytes 6758400 | tf_op jit(solution)/shard_map/reduce_scatter | solution.py:72
  27.3 8.5 %collective-permute-start = (bf16[1,8,32,1280]{3,1,2,0:T(8,128)(2,1)}, bf16[1,8,32,1280]{3,1,2,0:T(8,128)(2,1)}, u32[]{:S(2)}, u32[]{:S(2)}) collective-permute-start(bf16[1,8,32,1280]{3,1,2,0:T(8,128)(2,1)} %copy.47), channel_id=1, source_target_pairs={{0,1},{1,0},{2,3},{3,2},{4,5},{5,4},{6,7},{7,6},{8,9},{9,8},{10,11... | collective-permute-start | bytes 1966088 | tf_op jit(solution)/shard_map/ppermute | solution.py:22
  29.0 34.4 %collective-permute-start.1 = (bf16[1,8,32,1280]{3,1,2,0:T(8,128)(2,1)}, bf16[1,8,32,1280]{3,1,2,0:T(8,128)(2,1)}, u32[]{:S(2)}, u32[]{:S(2)}) collective-permute-start(bf16[1,8,32,1280]{3,1,2,0:T(8,128)(2,1)} %copy.48), channel_id=1, source_target_pairs={{0,2},{1,3},{2,0},{3,1},{4,6},{5,7},{6,4},{7,5},{8,10},{9,11},{10,... | collective-permute-start | bytes 1966088 | tf_op jit(solution)/shard_map/ppermute | solution.py:22
  32.7 43.1 %collective-permute-start.2 = (bf16[1,8,32,1280]{3,1,2,0:T(8,128)(2,1)}, bf16[1,8,32,1280]{3,1,2,0:T(8,128)(2,1)}, u32[]{:S(2)}, u32[]{:S(2)}) collective-permute-start(bf16[1,8,32,1280]{3,1,2,0:T(8,128)(2,1)} %copy.49), channel_id=1, source_target_pairs={{0,3},{1,2},{2,1},{3,0},{4,7},{5,6},{6,5},{7,4},{8,11},{9,10},{10,... | collective-permute-start | bytes 1966088 | tf_op jit(solution)/shard_map/ppermute | solution.py:22
  32.8 1.8 copy-start.1
  34.6 43.2 %copy-start.5 = (f32[32,32]{1,0:T(8,128)S(1)}, f32[32,32]{1,0:T(8,128)}, u32[]{:S(2)}) copy-start(f32[32,32]{1,0:T(8,128)} %param.7) | copy-start | bytes 12292
  34.6 43.2 %copy-start.6 = (f32[32]{0:T(128)S(1)}, f32[32]{0:T(128)}, u32[]{:S(2)}) copy-start(f32[32]{0:T(128)} %param.8) | copy-start | bytes 388
  122.5 2.7 copy-start.2
  122.8 1.5 copy-start.3
  140.9 102.2 %all-to-all-start.2 = ((bf16[1,32,32,1280]{3,2,0,1:T(8,128)(2,1)}), bf16[1,32,32,1280]{3,2,0,1:T(8,128)(2,1)}, u32[]{:S(2)}, u32[]{:S(2)}) async-start(bf16[1,32,32,1280]{3,2,0,1:T(8,128)(2,1)} %copy.42), calls=%async_computation.2 | async-start | bytes 5242880 | tf_op jit(solution)/shard_map/all_to_all | solution.py:71
  243.0 3.6 %copy-start.4 = (bf16[1,8,4,32,1280]{4,3,2,1,0:T(8,128)(2,1)S(1)}, bf16[1,8,4,32,1280]{4,3,2,1,0:T(8,128)(2,1)}, u32[]{:S(2)}) copy-start(bf16[1,8,4,32,1280]{4,3,2,1,0:T(8,128)(2,1)} %copy-done.3) | copy-start | bytes 7864324
  243.0 3.6 %copy-start.7 = (f32[1280]{0:T(1024)S(1)}, f32[1280]{0:T(1024)}, u32[]{:S(2)}) copy-start(f32[1280]{0:T(1024)} %param.10) | copy-start | bytes 15364
Sparse Core Ops, SparseCore 0:
  131.0 147.6 reduce-scatter.1
